TPU v7x, 1024 devices: a whole 4x4x32 slice. The times are simulated.
1024 devices in a mesh: pipe: 8 (over x, core), ctx: 8 (over z_lo), dp: 16 (over z_hi, y).
Axes of the slice: x: 4, y: 4, z: 32 (z_hi: 4, z_lo: 8; z = z_hi * 8 + z_lo), core: 2. Of those that a mesh axis runs over, the one named last changes fastest.
Arguments:
- section_held: bfloat16 [8, 16, 2048, 1024], P('pipe', 'dp', 'ctx'), may hold values from -6 to 6
- segments: int32 [8, 16, 2048], P('pipe', 'dp'), may hold values from 0 to 3, never falling along the last dimension, each value on 1 to 1024 neighbouring positions
- norm_gain: float32 [8, 1024], P('pipe'), may hold values from 0.1 to 1.9
- w_qkv: bfloat16 [8, 1024, 1536], P('pipe')
- w_out: bfloat16 [8, 512, 1024], P('pipe'), may hold values from -1 to 1
- grad_parts: float32 [8, 8, 16, 524288], P('pipe', 'ctx', 'dp'), may hold values from -2 to 2
- master: float32 [8, 524288], P('pipe', ('ctx', 'dp')), may hold values from -0.25 to 0.25
- moment: float32 [8, 524288], P('pipe', ('ctx', 'dp')), may hold values from -4 to 4
- second: float32 [8, 524288], P('pipe', ('ctx', 'dp')), may hold values from 0.1 to 1
Outputs:
- section_next: bfloat16 [8, 16, 2048, 1024], P('pipe', 'dp', 'ctx')
- new_master: float32 [8, 524288], P('pipe', ('ctx', 'dp'))
- new_moment: float32 [8, 524288], P('pipe', ('ctx', 'dp'))
- new_second: float32 [8, 524288], P('pipe', ('ctx', 'dp'))
Inputs may be any that keep to these rules, and one draw needn't show every extreme that they name: `segments`: within each sequence the ids never fall and each segment holds 1 to 1024 tokens.
All inputs are finite; a program needn't handle non-finite values.
Results may differ from a plain program's by a relative error of at most 0.006.
Values may be sent and summed in bfloat16 or wider, within the bound.
A program may use at most 64 MiB of HBM per device.

v0:
```python
import jax
import jax.numpy as jnp
from jax import lax
from jax.sharding import PartitionSpec as P

H = 4
DH = 128


eps_norm = 1e-06
rate = 0.001
beta_one = 0.9
beta_two = 0.999
adam_eps = 1e-08
decay = 0.1
fix_one = 0.9999734386011124
fix_two = 0.09520785288629038


def shifted(value, axis, by):
    count = lax.axis_size(axis)
    return lax.ppermute(value, axis, [(i, (i + by) % count) for i in range(count)])


def on_device(section_held, segments, norm_gain, w_qkv, w_out, grad_parts, master, moment, second):
    incoming = shifted(section_held, "pipe", 1)
    inputs = incoming[0, 0]
    row_count = inputs.shape[0]
    head_cols = H * DH
    values = inputs.astype(jnp.float32)
    meansq = jnp.mean(values * values, axis=-1, keepdims=True)
    normed = (values * lax.rsqrt(meansq + eps_norm) * norm_gain[0]).astype(jnp.bfloat16)
    projected = jnp.dot(normed, w_qkv[0], preferred_element_type=jnp.float32)
    queries = projected[:, :head_cols].astype(jnp.bfloat16).reshape(row_count, H, DH)
    key_rows = projected[:, head_cols : 2 * head_cols].astype(jnp.bfloat16)
    value_rows = projected[:, 2 * head_cols :].astype(jnp.bfloat16)
    seg_all = segments[0, 0]
    my_start = lax.axis_index("ctx") * row_count
    query_seg = lax.dynamic_slice_in_dim(seg_all, my_start, row_count)
    query_pos = my_start + jnp.arange(row_count, dtype=jnp.int32)
    score_scale = DH ** (-0.5)
    running = jnp.full((H, row_count), -1e30, jnp.float32)
    key_part = lax.all_gather(key_rows, "ctx", axis=0, tiled=True)
    value_part = lax.all_gather(value_rows, "ctx", axis=0, tiled=True)
    key_count = key_part.shape[0]
    key_heads = key_part.reshape(key_count, H, DH)
    value_heads = value_part.reshape(key_count, H, DH)
    scores = (
        jnp.einsum("qhd,khd->hqk", queries, key_heads, preferred_element_type=jnp.float32)
        * score_scale
    )
    key_pos = jnp.arange(key_count, dtype=jnp.int32)
    allowed = (key_pos[None, :] <= query_pos[:, None]) & (seg_all[None, :] == query_seg[:, None])
    scores = jnp.where(allowed[None], scores, -1e30)
    newest = jnp.maximum(running, jnp.max(scores, axis=-1))
    weights = jnp.where(allowed[None], jnp.exp(scores - newest[:, :, None]), 0.0)
    totals = jnp.sum(weights, axis=-1)
    weighted = jnp.einsum(
        "hqk,khd->hqd",
        weights.astype(jnp.bfloat16),
        value_heads,
        preferred_element_type=jnp.float32,
    )
    running, totals, weighted = (newest, totals, weighted)
    attended = (
        jnp.transpose(weighted / totals[:, :, None], (1, 0, 2))
        .reshape(row_count, head_cols)
        .astype(jnp.bfloat16)
    )
    section_next = (
        (jnp.dot(attended, w_out[0], preferred_element_type=jnp.float32) + values)
        .astype(jnp.bfloat16)
        .reshape(section_held.shape)
    )
    flat_grad = grad_parts.reshape(-1)
    grad_sum = lax.psum_scatter(flat_grad, ("ctx", "dp"), scatter_dimension=0, tiled=True)
    master_row = master[0]
    new_moment = beta_one * moment[0] + (1.0 - beta_one) * grad_sum
    new_second = beta_two * second[0] + (1.0 - beta_two) * grad_sum * grad_sum
    update = new_moment / fix_one / (jnp.sqrt(new_second / fix_two) + adam_eps) + decay * master_row
    new_master = master_row - rate * update
    return (
        section_next,
        new_master.reshape(master.shape),
        new_moment.reshape(moment.shape),
        new_second.reshape(second.shape),
    )


def solution(mesh):
    in_specs = (
        P("pipe", "dp", "ctx", None),
        P("pipe", "dp", None),
        P("pipe", None),
        P("pipe", None, None),
        P("pipe", None, None),
        P("pipe", "ctx", "dp", None),
        P("pipe", ("ctx", "dp")),
        P("pipe", ("ctx", "dp")),
        P("pipe", ("ctx", "dp")),
    )
    out_specs = (
        P("pipe", "dp", "ctx", None),
        P("pipe", ("ctx", "dp")),
        P("pipe", ("ctx", "dp")),
        P("pipe", ("ctx", "dp")),
    )
    return jax.shard_map(
        on_device, mesh=mesh, in_specs=in_specs, out_specs=out_specs, check_vma=False
    )
```

profile of v0, /device:TPU:6, one launch (start us, length us, event | category | flops | bytes accessed | tf_op | source)
XLA Modules:
  0.0 599.1 jit_solution(12386582241065292748)
XLA Ops:
  8.0 0.0 copy-start
  8.0 0.0 all-reduce.3.cloned.1.call-start
  8.1 0.7 all-reduce.3.cloned.1.call-update
  8.7 0.0 copy-start.9
  8.8 0.0 copy-start.7
  8.8 0.0 copy-start.8
  8.8 0.0 copy-start.6
  8.8 0.0 all-gather.3.cloned.1.call-start
  8.8 0.0 collective-permute-start
  8.9 8.8 %collective-permute-done = bf16[1,1,256,1024]{3,2,1,0:T(8,128)(2,1)S(1)} collective-permute-done((bf16[1,1,256,1024]{3,2,1,0:T(8,128)(2,1)}, bf16[1,1,256,1024]{3,2,1,0:T(8,128)(2,1)S(1)}, u32[]{:S(2)}, u32[]{:S(2)}) %collective-permute-start) | collective-permute-done | bytes 524320 | tf_op jit(solution)/shard_map/ppermute | solution.py:22
  17.7 0.2 fusion.21
  17.9 0.6 copy-done.3
  18.5 0.0 copy-done
  18.5 1.7 fusion.8
  20.2 0.9 slice_bitcast_fusion
  21.1 0.0 all-gather.3.cloned.1.call-update
  21.1 0.0 all-gather.5.cloned.1.call-start
  21.2 0.0 copy-done.9
  21.2 0.5 all-gather.5.cloned.1.call-update
  21.7 1.4 fusion.14
  23.1 1.3 dynamic-slice.1
  25.0 0.0 copy-done.7
  25.1 544.1 %all-reduce.3.cloned.1.call-done = f32[524288]{0:T(1024)} async-done(((f32[524288]{0:T(1024)}), f32[524288]{0:T(1024)}) %all-reduce.3.cloned.1.call-update) | async-done | bytes 2097168
  569.2 0.0 copy-done.6
  569.2 1.3 multiply_subtract_fusion
  570.5 3.6 fusion
  574.1 3.2 copy-done.1
  577.3 2.5 fusion.1
  579.8 0.0 all-gather.5.cloned.1.call-done
  579.8 4.0 copy.19
  583.8 6.6 %fusion.28 = bf16[256,4,128]{0,2,1:T(8,128)(2,1)S(1)} fusion(bf16[2048,4,128]{0,2,1:T(8,128)(2,1)} %bitcast.64, f32[4,256,2048]{2,1,0:T(8,128)} %copy-done.1, f32[4,256]{1,0:T(4,128)S(1)} %broadcast_maximum_fusion, pred[256,2048]{1,0:T(8,128)(4,1)} %fusion.14, f32[256,4]{0,1:T(4,128)S(1)} %bitcast.73), kind=kOutput, calls=%fused_computation.27 | convolution fusion | flops 547618816 | bytes 11280384 | tf_op jit(solution)/shard_map/hqk,khd->hqd/dot_general | solution.py:58
  590.4 1.3 fusion.17
  (16 shorter events, 0.1 us)
Async XLA Ops:
  8.0 10.5 %copy-start = (bf16[1,1024,1536]{2,1,0:T(8,128)(2,1)S(1)}, bf16[1,1024,1536]{2,1,0:T(8,128)(2,1)}, u32[]{:S(2)}) copy-start(bf16[1,1024,1536]{2,1,0:T(8,128)(2,1)} %param.12) | copy-start | bytes 9437188
  8.0 561.1 %all-reduce.3.cloned.1.call-start = ((), (), s32[]{:S(2)}) async-start(), calls=%async_computation.2 | async-start | bytes 4194304
  8.7 12.4 %copy-start.9 = (s32[1,1,2048]{2,1,0:T(1,128)S(1)}, s32[1,1,2048]{2,1,0:T(1,128)}, u32[]{:S(2)}) copy-start(s32[1,1,2048]{2,1,0:T(1,128)} %param.10) | copy-start | bytes 24580
  8.8 16.2 %copy-start.7 = (f32[1,4096]{1,0:T(1,128)S(1)}, f32[1,4096]{1,0:T(1,128)}, u32[]{:S(2)}) copy-start(f32[1,4096]{1,0:T(1,128)} %param.16) | copy-start | bytes 49156
  8.8 16.2 %copy-start.8 = (f32[1,4096]{1,0:T(1,128)S(1)}, f32[1,4096]{1,0:T(1,128)}, u32[]{:S(2)}) copy-start(f32[1,4096]{1,0:T(1,128)} %param.17) | copy-start | bytes 49156
  8.8 560.4 %copy-start.6 = (f32[1,4096]{1,0:T(1,128)S(1)}, f32[1,4096]{1,0:T(1,128)}, u32[]{:S(2)}) copy-start(f32[1,4096]{1,0:T(1,128)} %param.15) | copy-start | bytes 49156
  8.8 561.7 %all-gather.3.cloned.1.call-start = ((), (), s32[]{:S(2)}) async-start(), calls=%async_computation | async-start | bytes 2359296 | tf_op jit(solution)/shard_map/all_gather | solution.py:43
  8.8 8.8 %collective-permute-start = (bf16[1,1,256,1024]{3,2,1,0:T(8,128)(2,1)}, bf16[1,1,256,1024]{3,2,1,0:T(8,128)(2,1)S(1)}, u32[]{:S(2)}, u32[]{:S(2)}) collective-permute-start(bf16[1,1,256,1024]{3,2,1,0:T(8,128)(2,1)} %param.9), channel_id=1, source_target_pairs={{0,128},{128,256},{256,384},{384,512},{512,640},{640,768},{768,896... | collective-permute-start | bytes 1572872 | tf_op jit(solution)/shard_map/ppermute | solution.py:22
  17.7 0.8 copy-start.3
  21.1 558.7 %all-gather.5.cloned.1.call-start = ((), (), s32[]{:S(2)}) async-start(), calls=%async_computation.1 | async-start | bytes 2359296 | tf_op jit(solution)/shard_map/all_gather | solution.py:44
  570.5 6.8 %copy-start.2 = (pred[256,2048]{1,0:T(8,128)(4,1)S(1)}, pred[256,2048]{1,0:T(8,128)(4,1)}, u32[]{:S(2)}) copy-start(pred[256,2048]{1,0:T(8,128)(4,1)} %fusion.14) | copy-start | bytes 1572868
  574.1 3.2 copy-start.1
  583.8 6.6 %copy-start.4 = (bf16[1,1,256,1024]{3,2,1,0:T(8,128)(2,1)S(1)}, bf16[1,1,256,1024]{3,2,1,0:T(8,128)(2,1)}, u32[]{:S(2)}) copy-start(bf16[1,1,256,1024]{3,2,1,0:T(8,128)(2,1)} %copy-done.3) | copy-start | bytes 1572868
  583.8 6.6 %copy-start.5 = (bf16[1,512,1024]{2,1,0:T(8,128)(2,1)S(1)}, bf16[1,512,1024]{2,1,0:T(8,128)(2,1)}, u32[]{:S(2)}) copy-start(bf16[1,512,1024]{2,1,0:T(8,128)(2,1)} %param.13) | copy-start | bytes 3145732
Sparse Core Ops, SparseCore 0:
  12.2 556.8 all-reduce.2
Sparse Core Ops, SparseCore 1:
  21.2 90.1 all-gather.2
  113.9 79.1 all-gather.4
where the time goes:
time: 599 us
  waiting for transfers between devices  554 us (92%)
  between operations  16.3 us (3%)
  matrix products  13.2 us (2%)
  local copies, waits for them, and re-layouts  9.94 us (2%)
    unnamed x4, waiting for transfers between devices  545 us
  transfers between devices with their start and end apart: 4, of which 2 were waited for; matrix products, arithmetic and copies ran while one was open for 2% of the time, Pallas kernels for 0%

commit v1 on v0

v1 whole, which is shorter than its diff:
```python
import functools

import jax
import jax.numpy as jnp
from jax import lax
from jax.experimental import pallas as pl
from jax.experimental.pallas import tpu as pltpu
from jax.sharding import PartitionSpec as P

H = 4
DH = 128
D = 1024
ROWS = 256
HALF = 128
HC = H * DH
FAR = 4
NEG = -1e30

eps_norm = 1e-06
rate = 0.001
beta_one = 0.9
beta_two = 0.999
adam_eps = 1e-08
decay = 0.1
fix_one = 0.9999734386011124
fix_two = 0.09520785288629038

MESH = pl.DeviceIdType.MESH
F32 = jnp.float32
BF16 = jnp.bfloat16


def kernel(
    x_hbm, seg_hbm, gain_hbm, wqkv_hbm, wout_hbm, g_hbm, ma_hbm, mo_hbm, se_hbm,
    out_hbm, nma_hbm, nmo_hbm, nse_hbm,
    xin, nrm, wqkv, wout, gain, seg, segq, kv, qs, acc, ms, ls, ov,
    g, r1a, r1b, r2p, r2m, red, rp, rm, ma, mo, se,
    loc, osem, xs, xr, ys, yr, ks, kr, zps, zpr, zms, zmr,
):
    p, c, d = lax.axis_index("pipe"), lax.axis_index("ctx"), lax.axis_index("dp")
    zh, y = lax.div(d, 4), lax.rem(d, 4)
    z = zh * 8 + c
    yp, ym, y2 = lax.rem(y + 1, 4), lax.rem(y + 3, 4), lax.rem(y + 2, 4)
    nxt, prv = (lax.rem(p + 1, 8), c, d), (lax.rem(p + 7, 8), c, d)
    dev_yp, dev_ym = (p, c, zh * 4 + yp), (p, c, zh * 4 + ym)
    up = (p, lax.rem(c + 1, 8), lax.rem(zh + lax.div(c + 1, 8), 4) * 4 + y)
    down = (p, lax.rem(c + 7, 8), lax.rem(zh + 3 + lax.div(c + 7, 8), 4) * 4 + y)

    def remote(src, dst, ssem, rsem, dev):
        return pltpu.make_async_remote_copy(
            src_ref=src, dst_ref=dst, send_sem=ssem, recv_sem=rsem, device_id=dev, device_id_type=MESH
        )

    local = [
        pltpu.make_async_copy(a, b, loc.at[i])
        for i, (a, b) in enumerate(
            [(seg_hbm, seg), (gain_hbm, gain), (wqkv_hbm, wqkv), (g_hbm, g), (wout_hbm, wout),
             (ma_hbm, ma), (mo_hbm, mo), (se_hbm, se)]
        )
    ]
    for one in local:
        one.start()

    barrier = pltpu.get_barrier_semaphore()
    for dev in (nxt, prv, dev_yp, dev_ym, up, down):
        pl.semaphore_signal(barrier, inc=1, device_id=dev, device_id_type=MESH)
    pl.semaphore_wait(barrier, 6)

    def x_copy(r):
        rows = pl.ds(r * HALF, HALF)
        return remote(x_hbm.at[rows], xin.at[rows], xs.at[r], xr.at[r], nxt)

    y_one = [
        remote(g_hbm.at[pl.ds(0, 4), :, y2], r1a, ys.at[0], yr.at[0], dev_yp),
        remote(g_hbm.at[pl.ds(4, 4), :, y2], r1b, ys.at[1], yr.at[1], dev_ym),
    ]
    y_two = [
        remote(g_hbm.at[pl.ds(4, 4), :, yp], r2p.at[pl.ds(4, 4)], ys.at[2], yr.at[2], dev_yp),
        remote(g_hbm.at[pl.ds(0, 4), :, ym], r2m.at[pl.ds(0, 4)], ys.at[3], yr.at[3], dev_ym),
    ]
    y_sum = [
        remote(r1a, r2p.at[pl.ds(0, 4)], ys.at[4], yr.at[4], dev_yp),
        remote(r1b, r2m.at[pl.ds(4, 4)], ys.at[5], yr.at[5], dev_ym),
    ]
    for r in range(2):
        x_copy(r).start()
    for one in (*y_one, *y_two):
        one.start()

    def kv_copy(k, r):
        return remote(kv.at[k, r], kv.at[k + 1, r], ks.at[k, r], kr.at[k, r], up)

    def project(r):
        rows = pl.ds(r * HALF, HALF)
        x_copy(r).wait_recv()
        values = xin[rows, :].astype(F32)
        meansq = jnp.mean(values * values, axis=-1, keepdims=True)
        normed = (values * lax.rsqrt(meansq + eps_norm) * gain[...]).astype(BF16)
        nrm[rows, :] = normed
        both = jnp.dot(normed, wqkv[:, HC:], preferred_element_type=F32).astype(BF16)
        for t in range(2):
            for h in range(H):
                kv[0, r, t, h] = both[:, t * HC + h * DH : t * HC + (h + 1) * DH]

        @pl.when(c < 7)
        def _():
            kv_copy(0, r).start()


    def attend(k, r, q0, qn, causal=False):
        rows = pl.ds(q0, qn)
        keyseg = seg[pl.ds(2 * (c - k) + r, 1), :]
        mask = segq[rows, :] == keyseg
        if causal:
            place = lax.broadcasted_iota(jnp.int32, (qn, HALF), 0) + q0
            mask = mask & (lax.broadcasted_iota(jnp.int32, (qn, HALF), 1) + r * HALF <= place)
        for h in range(H):
            s = lax.dot_general(
                qs[h, rows, :], kv[k, r, 0, h], (((1,), (1,)), ((), ())), preferred_element_type=F32
            )
            s = jnp.where(mask, s * (DH ** (-0.5)), NEG)
            old = ms[h, rows, :]
            top = jnp.maximum(old, jnp.max(s, axis=-1, keepdims=True))
            w = jnp.exp(s - top)
            shrink = jnp.exp(old - top)
            ms[h, rows, :] = top
            ls[h, rows, :] = shrink * ls[h, rows, :] + jnp.sum(w, axis=-1, keepdims=True)
            acc[h, rows, :] = shrink * acc[h, rows, :] + jnp.dot(
                w.astype(BF16), kv[k, r, 1, h], preferred_element_type=F32
            )

    def arrived(k, r):
        @pl.when(c >= k)
        def _():
            kv_copy(k - 1, r).wait_recv()

        if k < FAR:
            @pl.when((c >= k) & (c < 7))
            def _():
                kv_copy(k, r).start()

        @pl.when(c >= k)
        def _():
            if k == FAR and r == 0:
                attend(k, r, 0, HALF)
            else:
                attend(k, r, 0, ROWS)

    def shard(t):
        return lax.rem(t, 8), lax.div(t, 8)

    def up_copy(i):
        if i == 0:
            a, b = shard(lax.rem(z + 16, 32))
            src = red.at[a, b]
        else:
            src = rp.at[i - 1]
        return remote(src, rp.at[i], zps.at[i], zpr.at[i], up)

    def down_copy(i):
        if i == 0:
            a, b = shard(lax.rem(z + 17, 32))
            src = red.at[a, b]
        else:
            src = rm.at[i - 1]
        return remote(src, rm.at[i], zms.at[i], zmr.at[i], down)

    def ring(i):
        up_copy(i - 1).wait_recv()
        a, b = shard(lax.rem(z + 16 - i + 32, 32))
        rp[i - 1] = rp[i - 1] + red[a, b]
        up_copy(i).start()
        if i < 15:
            down_copy(i - 1).wait_recv()
            a, b = shard(lax.rem(z + 17 + i, 32))
            rm[i - 1] = rm[i - 1] + red[a, b]
            down_copy(i).start()

    for i in (0, 1, 2):
        local[i].wait()
    project(0)
    for r in range(2):
        cols = jnp.broadcast_to(seg[pl.ds(2 * c + r, 1), :], (HALF, HALF))
        segq[pl.ds(r * HALF, HALF), :] = jnp.transpose(cols)
    project(1)
    local[3].wait()
    y_one[0].wait_recv()
    r1a[...] = r1a[...] + g[pl.ds(0, 4), :, yp]
    y_sum[0].start()
    y_one[1].wait_recv()
    r1b[...] = r1b[...] + g[pl.ds(4, 4), :, ym]
    y_sum[1].start()

    queries = jnp.dot(nrm[...], wqkv[:, :HC], preferred_element_type=F32).astype(BF16)
    for h in range(H):
        qs[h] = queries[:, h * DH : (h + 1) * DH]
    ms[...] = jnp.full_like(ms, NEG)
    ls[...] = jnp.zeros_like(ls)
    acc[...] = jnp.zeros_like(acc)
    attend(0, 0, 0, ROWS, causal=True)
    attend(0, 1, HALF, HALF, causal=True)
    arrived(1, 0)

    for one in (*y_two, *y_sum):
        one.wait_recv()
    red[...] = g[:, :, y] + r2p[...] + r2m[...]
    up_copy(0).start()
    down_copy(0).start()
    arrived(1, 1)
    plan = {3: (2, 0), 6: (2, 1), 9: (3, 0), 12: (3, 1)}
    for i in range(1, 16):
        ring(i)
        if i in plan:
            arrived(*plan[i])
    for i in (5, 6, 7):
        local[i].wait()
    up_copy(15).wait_recv()
    down_copy(14).wait_recv()
    grad = red[c, zh] + rp[15] + rm[14]
    new_moment = beta_one * mo[...] + (1.0 - beta_one) * grad
    new_second = beta_two * se[...] + (1.0 - beta_two) * grad * grad
    update = new_moment / fix_one / (jnp.sqrt(new_second / fix_two) + adam_eps) + decay * ma[...]
    ma[...] = ma[...] - rate * update
    mo[...] = new_moment
    se[...] = new_second
    outs = [
        pltpu.make_async_copy(a, b, osem.at[i])
        for i, (a, b) in enumerate([(ma, nma_hbm), (mo, nmo_hbm), (se, nse_hbm), (ov, out_hbm)])
    ]
    for one in outs[:3]:
        one.start()
    local[4].wait()
    arrived(4, 0)
    arrived(4, 1)

    heads = [(acc[h] / ls[h]).astype(BF16) for h in range(H)]
    attended = jnp.concatenate(heads, axis=1)
    final = jnp.dot(attended, wout[...], preferred_element_type=F32) + xin[...].astype(F32)
    ov[...] = final.astype(BF16)
    outs[3].start()

    for r in range(2):
        x_copy(r).wait_send()
    for one in (*y_one, *y_two, *y_sum):
        one.wait_send()
    for i in range(16):
        up_copy(i).wait_send()
    for i in range(15):
        down_copy(i).wait_send()
    for k in range(FAR):
        @pl.when((c >= k) & (c < 7))
        def _():
            for r in range(2):
                kv_copy(k, r).wait_send()
    for one in outs:
        one.wait()


def on_device(section_held, segments, norm_gain, w_qkv, w_out, grad_parts, master, moment, second):
    shard_rows = (32, 128)
    any_spec = pl.BlockSpec(memory_space=pl.ANY)
    vmem, dma = pltpu.VMEM, pltpu.SemaphoreType.DMA
    outs = pl.pallas_call(
        kernel,
        out_shape=(
            jax.ShapeDtypeStruct((ROWS, D), BF16),
            jax.ShapeDtypeStruct(shard_rows, F32),
            jax.ShapeDtypeStruct(shard_rows, F32),
            jax.ShapeDtypeStruct(shard_rows, F32),
        ),
        in_specs=[any_spec] * 9,
        out_specs=[any_spec] * 4,
        scratch_shapes=[
            vmem((ROWS, D), BF16),
            vmem((ROWS, D), BF16),
            vmem((D, 3 * HC), BF16),
            vmem((HC, D), BF16),
            vmem((1, D), F32),
            vmem((16, 128), jnp.int32),
            vmem((ROWS, HALF), jnp.int32),
            vmem((FAR + 1, 2, 2, H, HALF, DH), BF16),
            vmem((H, ROWS, DH), BF16),
            vmem((H, ROWS, DH), F32),
            vmem((H, ROWS, DH), F32),
            vmem((H, ROWS, DH), F32),
            vmem((ROWS, D), BF16),
            vmem((8, 4, 4, 32, 128), F32),
            vmem((4, 4, 32, 128), F32),
            vmem((4, 4, 32, 128), F32),
            vmem((8, 4, 32, 128), F32),
            vmem((8, 4, 32, 128), F32),
            vmem((8, 4, 32, 128), F32),
            vmem((16, 32, 128), F32),
            vmem((15, 32, 128), F32),
            vmem(shard_rows, F32),
            vmem(shard_rows, F32),
            vmem(shard_rows, F32),
            dma((8,)), dma((4,)),
            dma((2,)), dma((2,)),
            dma((6,)), dma((6,)),
            dma((FAR, 2)), dma((FAR, 2)),
            dma((16,)), dma((16,)),
            dma((15,)), dma((15,)),
        ],
        compiler_params=pltpu.CompilerParams(
            collective_id=0, has_side_effects=True, vmem_limit_bytes=48 << 20
        ),
    )(
        section_held.reshape(ROWS, D),
        segments.reshape(16, 128),
        norm_gain,
        w_qkv[0],
        w_out[0],
        grad_parts.reshape(8, 4, 4, 32, 128),
        master.reshape(shard_rows),
        moment.reshape(shard_rows),
        second.reshape(shard_rows),
    )
    return (
        outs[0].reshape(section_held.shape),
        outs[1].reshape(master.shape),
        outs[2].reshape(moment.shape),
        outs[3].reshape(second.shape),
    )


def solution(mesh):
    in_specs = (
        P("pipe", "dp", "ctx", None),
        P("pipe", "dp", None),
        P("pipe", None),
        P("pipe", None, None),
        P("pipe", None, None),
        P("pipe", "ctx", "dp", None),
        P("pipe", ("ctx", "dp")),
        P("pipe", ("ctx", "dp")),
        P("pipe", ("ctx", "dp")),
    )
    out_specs = (
        P("pipe", "dp", "ctx", None),
        P("pipe", ("ctx", "dp")),
        P("pipe", ("ctx", "dp")),
        P("pipe", ("ctx", "dp")),
    )
    return jax.shard_map(
        on_device, mesh=mesh, in_specs=in_specs, out_specs=out_specs, check_vma=False
    )
```

time: 599 us -> 106 us (0.18)
  waiting for transfers between devices: 554 us -> 0 us
  Pallas kernels: 0 us -> 93.8 us
  between operations: 16.3 us -> 0.66 us
  matrix products: 13.2 us -> 0 us
    unnamed x4 -> x0, waiting for transfers between devices: 545 us -> none
    pallas_call x0 -> x1, Pallas kernels: none -> 93.8 us  [on_device(): pl.pallas_call(kernel, out_shape=(jax.ShapeDtypeStruct((ROWS, D), BF16),...]
    dot_general x4 -> x0, matrix products: 13.2 us -> none  [the longest x1 6.6 us: on_device(): jnp.einsum('hqk,khd->hqd', weights.astype(jnp.bfloat16), value_heads, pre...]
    ppermute x1 -> x0, waiting for transfers between devices: 8.8 us -> none  [shifted(): lax.ppermute(value, axis, [(i, (i + by) % count) for i in range(count)])]
  transfers between devices with their start and end apart: 4 -> 0, of which waited for: 2 -> 0; matrix products, arithmetic and copies ran while one was open for 2% -> 0% of each run, Pallas kernels for 0% -> 0%
where the time goes in v1:
time: 106 us; the launch traced here: 104 us
  Pallas kernels  93.8 us (88%)
  local copies, waits for them, and re-layouts  9.99 us (9%)
    pallas_call x1, Pallas kernels, on_device(): pl.pallas_call(kernel, out_shape=(jax.ShapeDtypeStruct((ROWS, D), BF16),...  93.8 us
    unnamed x20, local copies, waits for them, and re-layouts  9.99 us

profile of v1, /device:TPU:6, one launch (start us, length us, event | category | flops | bytes accessed | tf_op | source)
XLA Modules:
  0.0 104.5 jit_solution(12118470207627356214)
XLA Ops:
  0.6 0.0 copy-start
  0.6 1.6 %copy-done = f32[1,1,1,524288]{3,2,1,0:T(1,128)S(1)} copy-done((f32[1,1,1,524288]{3,2,1,0:T(1,128)S(1)}, f32[1,1,1,524288]{3,2,1,0:T(1,128)}, u32[]{:S(2)}) %copy-start) | copy-done | bytes 2097176
  2.2 0.0 copy-start.1
  2.2 1.2 %copy-done.1 = bf16[1,512,1024]{2,1,0:T(8,128)(2,1)S(1)} copy-done((bf16[1,512,1024]{2,1,0:T(8,128)(2,1)S(1)}, bf16[1,512,1024]{2,1,0:T(8,128)(2,1)}, u32[]{:S(2)}) %copy-start.1) | copy-done | bytes 1048600
  3.5 0.0 copy-start.2
  3.5 1.0 copy-done.2
  4.5 0.0 copy-start.3
  4.5 0.7 copy-done.3
  5.2 0.0 copy-start.4
  5.2 0.7 copy-done.4
  5.9 0.0 copy-start.5
  5.9 0.7 copy-done.5
  6.6 0.0 copy-start.6
  6.6 0.7 copy-done.6
  7.3 0.0 copy-start.7
  7.3 0.7 copy-done.7
  8.0 93.8 %shard_map.120 = (bf16[256,1024]{1,0:T(8,128)(2,1)S(1)}, f32[32,128]{1,0:T(8,128)S(1)}, f32[32,128]{1,0:T(8,128)S(1)}, f32[32,128]{1,0:T(8,128)S(1)}) custom-call(bf16[256,1024]{1,0:T(8,128)(2,1)S(1)} %bitcast.14, s32[16,128]{1,0:T(8,128)S(1)} %bitcast.22, f32[1,1024]{1,0:T(1,128)S(1)} %copy-done.7, bf16[1024,1536]{1,0:T(8,128)(2,1)} %bitcast.23, ...), custom_call_target="tpu_custom_call" | custom-call | tf_op jit(solution)/shard_map/pallas_call | solution.py:263
  101.9 0.8 copy.17
  102.7 0.6 copy.18
  103.3 0.6 copy.19
  103.9 0.6 copy.20
Async XLA Ops:
  0.6 1.6 %copy-start = (f32[1,1,1,524288]{3,2,1,0:T(1,128)S(1)}, f32[1,1,1,524288]{3,2,1,0:T(1,128)}, u32[]{:S(2)}) copy-start(f32[1,1,1,524288]{3,2,1,0:T(1,128)} %param.14) | copy-start | bytes 6291460
  2.2 1.2 %copy-start.1 = (bf16[1,512,1024]{2,1,0:T(8,128)(2,1)S(1)}, bf16[1,512,1024]{2,1,0:T(8,128)(2,1)}, u32[]{:S(2)}) copy-start(bf16[1,512,1024]{2,1,0:T(8,128)(2,1)} %param.13) | copy-start | bytes 3145732
  3.5 1.0 copy-start.2
  4.5 0.7 copy-start.3
  5.2 0.7 copy-start.4
  5.9 0.7 copy-start.5
  6.6 0.7 copy-start.6
  7.3 0.7 copy-start.7

commit v2 on v1

v2 whole, which is shorter than its diff:
```python
import functools

import jax
import jax.numpy as jnp
from jax import lax
from jax.experimental import pallas as pl
from jax.experimental.pallas import tpu as pltpu
from jax.sharding import PartitionSpec as P

H = 4
DH = 128
D = 1024
ROWS = 256
HALF = 128
HC = H * DH
FAR_ORDER = (4, 3, 5, 2, 6, 1, 7)
FAR = 4
NEG = -1e30

eps_norm = 1e-06
rate = 0.001
beta_one = 0.9
beta_two = 0.999
adam_eps = 1e-08
decay = 0.1
fix_one = 0.9999734386011124
fix_two = 0.09520785288629038

MESH = pl.DeviceIdType.MESH
F32 = jnp.float32
BF16 = jnp.bfloat16


def kernel(
    x_hbm, seg_hbm, gain_hbm, wqkv_hbm, wout_hbm, g_hbm, ma_hbm, mo_hbm, se_hbm,
    ov, nma, nmo, nse,
    xin, nrm, wqkv, wout, gain, seg, segq, kv, qs, acc, ms, ls,
    g, yin, red, win, far, ma, mo, se,
    loc, xs, xr, ys, yr, ks, kr, ws, wr, fs, fr,
):
    p, c, d = lax.axis_index("pipe"), lax.axis_index("ctx"), lax.axis_index("dp")
    zh, y = lax.div(d, 4), lax.rem(d, 4)
    z = zh * 8 + c
    nxt, prv = (lax.rem(p + 1, 8), c, d), (lax.rem(p + 7, 8), c, d)

    def along_y(by):
        return p, c, zh * 4 + lax.rem(y + by, 4)

    def along_z(by):
        at = lax.rem(z + by + 32, 32)
        return p, lax.rem(at, 8), lax.div(at, 8) * 4 + y

    up = along_z(1)

    def remote(src, dst, ssem, rsem, dev):
        return pltpu.make_async_remote_copy(
            src_ref=src, dst_ref=dst, send_sem=ssem, recv_sem=rsem, device_id=dev, device_id_type=MESH
        )

    local = [
        pltpu.make_async_copy(a, b, loc.at[i])
        for i, (a, b) in enumerate(
            [(seg_hbm, seg), (gain_hbm, gain), (wqkv_hbm, wqkv), (g_hbm, g), (wout_hbm, wout),
             (ma_hbm, ma), (mo_hbm, mo), (se_hbm, se)]
        )
    ]
    for one in local:
        one.start()

    barrier = pltpu.get_barrier_semaphore()
    peers = [nxt, prv] + [along_y(i) for i in (1, 2, 3)]
    peers += [along_z(i) for i in (1, 2, 3, -1, -2, -3)] + [along_z(4 * i) for i in range(1, 8)]
    for dev in peers:
        pl.semaphore_signal(barrier, inc=1, device_id=dev, device_id_type=MESH)
    pl.semaphore_wait(barrier, len(peers))

    def x_copy(r):
        rows = pl.ds(r * HALF, HALF)
        return remote(x_hbm.at[rows], xin.at[rows], xs.at[r], xr.at[r], nxt)

    def group(j):
        return lax.rem(z + 1 + j, 4)

    def y_copy(j, i):
        src = g_hbm.at[:, group(j), :, lax.rem(y + i, 4)]
        return remote(src, yin.at[j, i - 1], ys.at[j, i - 1], yr.at[j, i - 1], along_y(i))

    for r in range(2):
        x_copy(r).start()
    for j in range(4):
        for i in (1, 2, 3):
            y_copy(j, i).start()

    def kv_copy(k, r):
        return remote(kv.at[k, r], kv.at[k + 1, r], ks.at[k, r], kr.at[k, r], up)

    def project(r):
        rows = pl.ds(r * HALF, HALF)
        x_copy(r).wait_recv()
        values = xin[rows, :].astype(F32)
        meansq = jnp.mean(values * values, axis=-1, keepdims=True)
        normed = (values * lax.rsqrt(meansq + eps_norm) * gain[...]).astype(BF16)
        nrm[rows, :] = normed
        both = jnp.dot(normed, wqkv[:, HC:], preferred_element_type=F32).astype(BF16)
        for t in range(2):
            for h in range(H):
                kv[0, r, t, h] = both[:, t * HC + h * DH : t * HC + (h + 1) * DH]

        @pl.when(c < 7)
        def _():
            kv_copy(0, r).start()


    def attend(k, r, q0, qn, causal=False):
        rows = pl.ds(q0, qn)
        keyseg = seg[pl.ds(2 * (c - k) + r, 1), :]
        mask = segq[rows, :] == keyseg
        if causal:
            place = lax.broadcasted_iota(jnp.int32, (qn, HALF), 0) + q0
            mask = mask & (lax.broadcasted_iota(jnp.int32, (qn, HALF), 1) + r * HALF <= place)
        for h in range(H):
            s = lax.dot_general(
                qs[h, rows, :], kv[k, r, 0, h], (((1,), (1,)), ((), ())), preferred_element_type=F32
            )
            s = jnp.where(mask, s * (DH ** (-0.5)), NEG)
            old = ms[h, rows, :]
            top = jnp.maximum(old, jnp.max(s, axis=-1, keepdims=True))
            w = jnp.exp(s - top)
            shrink = jnp.exp(old - top)
            ms[h, rows, :] = top
            ls[h, rows, :] = shrink * ls[h, rows, :] + jnp.sum(w, axis=-1, keepdims=True)
            acc[h, rows, :] = shrink * acc[h, rows, :] + jnp.dot(
                w.astype(BF16), kv[k, r, 1, h], preferred_element_type=F32
            )

    def arrived(k, r):
        @pl.when(c >= k)
        def _():
            kv_copy(k - 1, r).wait_recv()

        if k < FAR:
            @pl.when((c >= k) & (c < 7))
            def _():
                kv_copy(k, r).start()

        @pl.when(c >= k)
        def _():
            if k == FAR and r == 0:
                attend(k, r, 0, HALF)
            else:
                attend(k, r, 0, ROWS)

    def w_copy(j):
        return remote(red.at[j], win.at[j], ws.at[j], wr.at[j], along_z(j - 3))

    def y_sum(j):
        for i in (1, 2, 3):
            y_copy(j, i).wait_recv()
        red[j] = g[:, group(j), :, y] + yin[j, 0] + yin[j, 1] + yin[j, 2]
        if j < 3:
            w_copy(j).start()

    def f_copy(i):
        at = lax.rem(z + 32 - 4 * i, 32)
        src = red.at[3, lax.div(lax.rem(at, 8), 4), lax.div(at, 8)]
        return remote(src, far.at[i - 1], fs.at[i - 1], fr.at[i - 1], along_z(-4 * i))

    def w_sum():
        for j in range(3):
            w_copy(j).wait_recv()
        red[3] = red[3] + win[0] + win[1] + win[2]
        for i in FAR_ORDER:
            f_copy(i).start()

    for i in (0, 1, 2):
        local[i].wait()
    project(0)
    for r in range(2):
        cols = jnp.broadcast_to(seg[pl.ds(2 * c + r, 1), :], (HALF, HALF))
        segq[pl.ds(r * HALF, HALF), :] = jnp.transpose(cols)
    project(1)
    queries = jnp.dot(nrm[...], wqkv[:, :HC], preferred_element_type=F32).astype(BF16)
    for h in range(H):
        qs[h] = queries[:, h * DH : (h + 1) * DH]
    local[3].wait()
    y_sum(0)
    ms[...] = jnp.full_like(ms, NEG)
    ls[...] = jnp.zeros_like(ls)
    acc[...] = jnp.zeros_like(acc)
    attend(0, 0, 0, ROWS, causal=True)
    attend(0, 1, HALF, HALF, causal=True)
    arrived(1, 0)
    y_sum(1)
    arrived(1, 1)
    y_sum(2)
    arrived(2, 0)
    y_sum(3)
    arrived(2, 1)
    w_sum()
    arrived(3, 0)
    arrived(3, 1)
    arrived(4, 0)
    for i in (5, 6, 7):
        local[i].wait()
    for i in range(1, 8):
        f_copy(i).wait_recv()
    grad = red[3, lax.div(c, 4), zh]
    for i in range(7):
        grad = grad + far[i]
    new_moment = beta_one * mo[...] + (1.0 - beta_one) * grad
    new_second = beta_two * se[...] + (1.0 - beta_two) * grad * grad
    update = new_moment / fix_one / (jnp.sqrt(new_second / fix_two) + adam_eps) + decay * ma[...]
    nma[...] = ma[...] - rate * update
    nmo[...] = new_moment
    nse[...] = new_second
    local[4].wait()
    arrived(4, 1)

    heads = [(acc[h] / ls[h]).astype(BF16) for h in range(H)]
    attended = jnp.concatenate(heads, axis=1)
    final = jnp.dot(attended, wout[...], preferred_element_type=F32) + xin[...].astype(F32)
    ov[...] = final.astype(BF16)

    for r in range(2):
        x_copy(r).wait_send()
    for j in range(4):
        for i in (1, 2, 3):
            y_copy(j, i).wait_send()
    for j in range(3):
        w_copy(j).wait_send()
    for i in range(1, 8):
        f_copy(i).wait_send()
    for k in range(FAR):
        @pl.when((c >= k) & (c < 7))
        def _():
            for r in range(2):
                kv_copy(k, r).wait_send()


def hand_over(*refs):
    sems = refs[8]
    copies = [pltpu.make_async_copy(refs[i], refs[4 + i], sems.at[i]) for i in range(4)]
    for one in copies:
        one.start()
    for one in copies:
        one.wait()


def on_device(section_held, segments, norm_gain, w_qkv, w_out, grad_parts, master, moment, second):
    shard_rows = (32, 128)
    any_spec = pl.BlockSpec(memory_space=pl.ANY)
    vmem_spec = pl.BlockSpec(memory_space=pltpu.VMEM)
    vmem, dma = pltpu.VMEM, pltpu.SemaphoreType.DMA
    outs = pl.pallas_call(
        kernel,
        out_shape=(
            vmem((ROWS, D), BF16),
            vmem(shard_rows, F32),
            vmem(shard_rows, F32),
            vmem(shard_rows, F32),
        ),
        in_specs=[pl.BlockSpec(memory_space=pltpu.HBM)] * 9,
        out_specs=[vmem_spec] * 4,
        scratch_shapes=[
            vmem((ROWS, D), BF16),
            vmem((ROWS, D), BF16),
            vmem((D, 3 * HC), BF16),
            vmem((HC, D), BF16),
            vmem((1, D), F32),
            vmem((16, 128), jnp.int32),
            vmem((ROWS, HALF), jnp.int32),
            vmem((FAR + 1, 2, 2, H, HALF, DH), BF16),
            vmem((H, ROWS, DH), BF16),
            vmem((H, ROWS, DH), F32),
            vmem((H, ROWS, DH), F32),
            vmem((H, ROWS, DH), F32),
            vmem((2, 4, 4, 4, 32, 128), F32),
            vmem((4, 3, 2, 4, 32, 128), F32),
            vmem((4, 2, 4, 32, 128), F32),
            vmem((3, 2, 4, 32, 128), F32),
            vmem((7, 32, 128), F32),
            vmem(shard_rows, F32),
            vmem(shard_rows, F32),
            vmem(shard_rows, F32),
            dma((8,)),
            dma((2,)), dma((2,)),
            dma((4, 3)), dma((4, 3)),
            dma((FAR, 2)), dma((FAR, 2)),
            dma((3,)), dma((3,)),
            dma((7,)), dma((7,)),
        ],
        compiler_params=pltpu.CompilerParams(
            collective_id=0, has_side_effects=True, vmem_limit_bytes=48 << 20
        ),
    )(
        *(pltpu.with_memory_space_constraint(one, pltpu.HBM) for one in (
            section_held.reshape(ROWS, D),
            segments.reshape(16, 128),
            norm_gain,
            w_qkv[0],
            w_out[0],
            grad_parts.reshape(2, 4, 4, 4, 32, 128),
            master.reshape(shard_rows),
            moment.reshape(shard_rows),
            second.reshape(shard_rows),
        ))
    )
    outs = pl.pallas_call(
        hand_over,
        out_shape=[jax.ShapeDtypeStruct(one.shape, one.dtype) for one in outs],
        in_specs=[any_spec] * 4,
        out_specs=[any_spec] * 4,
        scratch_shapes=[dma((4,))],
        compiler_params=pltpu.CompilerParams(vmem_limit_bytes=4 << 20),
    )(*outs)
    return (
        outs[0].reshape(section_held.shape),
        outs[1].reshape(master.shape),
        outs[2].reshape(moment.shape),
        outs[3].reshape(second.shape),
    )


def solution(mesh):
    in_specs = (
        P("pipe", "dp", "ctx", None),
        P("pipe", "dp", None),
        P("pipe", None),
        P("pipe", None, None),
        P("pipe", None, None),
        P("pipe", "ctx", "dp", None),
        P("pipe", ("ctx", "dp")),
        P("pipe", ("ctx", "dp")),
        P("pipe", ("ctx", "dp")),
    )
    out_specs = (
        P("pipe", "dp", "ctx", None),
        P("pipe", ("ctx", "dp")),
        P("pipe", ("ctx", "dp")),
        P("pipe", ("ctx", "dp")),
    )
    return jax.shard_map(
        on_device, mesh=mesh, in_specs=in_specs, out_specs=out_specs, check_vma=False
    )
```

time: 106 us -> 88.2 us (0.83)
  the two profiles are of different devices: /device:TPU:6 before, /device:TPU:152 now
where the time goes in v2:
time: 88.2 us; the launch traced here: 88.1 us
  Pallas kernels  87.4 us (99%)
    pallas_call x1, Pallas kernels, on_device(): pl.pallas_call(kernel, out_shape=(vmem((ROWS, D), BF16), vmem(shard_rows,...  86.6 us

profile of v2, /device:TPU:152, one launch (start us, length us, event | category | flops | bytes accessed | tf_op | source)
XLA Modules:
  0.0 88.1 jit_solution(9423674554646662378)
XLA Ops:
  0.6 86.6 %shard_map.120 = (bf16[256,1024]{1,0:T(8,128)(2,1)S(1)}, f32[32,128]{1,0:T(8,128)S(1)}, f32[32,128]{1,0:T(8,128)S(1)}, f32[32,128]{1,0:T(8,128)S(1)}) custom-call(bf16[256,1024]{1,0:T(8,128)(2,1)} %bitcast.15, s32[16,128]{1,0:T(8,128)} %bitcast.19, f32[1,1024]{1,0:T(1,128)} %gain_hbm.1, bf16[1024,1536]{1,0:T(8,128)(2,1)} %bitcast.12, ...), custom_call_target="tpu_custom_call" | custom-call | tf_op jit(solution)/shard_map/pallas_call | solution.py:254
  87.2 0.8 shard_map.121

commit v3 on v2

--- a/solution.py
+++ b/solution.py
@@ -36,7 +36,7 @@
     ov, nma, nmo, nse,
     xin, nrm, wqkv, wout, gain, seg, segq, kv, qs, acc, ms, ls,
     g, yin, red, win, far, ma, mo, se,
-    loc, xs, xr, ys, yr, ks, kr, ws, wr, fs, fr,
+    loc, xs, xr, ys, yr, ks, kr, ws, wr, fs, fr, said,
 ):
     p, c, d = lax.axis_index("pipe"), lax.axis_index("ctx"), lax.axis_index("dp")
     zh, y = lax.div(d, 4), lax.rem(d, 4)
@@ -68,18 +68,24 @@
         one.start()
 
     barrier = pltpu.get_barrier_semaphore()
-    peers = [nxt, prv] + [along_y(i) for i in (1, 2, 3)]
-    peers += [along_z(i) for i in (1, 2, 3, -1, -2, -3)] + [along_z(4 * i) for i in range(1, 8)]
-    for dev in peers:
+    for dev in (prv, along_y(1), along_y(2), along_y(3), along_z(-1)):
         pl.semaphore_signal(barrier, inc=1, device_id=dev, device_id_type=MESH)
-    pl.semaphore_wait(barrier, len(peers))
+    pl.semaphore_wait(barrier, 5)
+    pl.semaphore_signal(said.at[0], inc=1, device_id=up, device_id_type=MESH)
+
+    def known(i):
+        pl.semaphore_wait(said.at[i], 1 if i == 0 else 2)
+        if i < 6:
+            far_by = 1 if i < 3 else 4
+            for by in (far_by, -far_by):
+                pl.semaphore_signal(said.at[i + 1], inc=1, device_id=along_z(by), device_id_type=MESH)
 
     def x_copy(r):
         rows = pl.ds(r * HALF, HALF)
         return remote(x_hbm.at[rows], xin.at[rows], xs.at[r], xr.at[r], nxt)
 
     def group(j):
-        return lax.rem(z + 1 + j, 4)
+        return lax.rem(z + 3 - j, 4)
 
     def y_copy(j, i):
         src = g_hbm.at[:, group(j), :, lax.rem(y + i, 4)]
@@ -151,7 +157,7 @@
                 attend(k, r, 0, ROWS)
 
     def w_copy(j):
-        return remote(red.at[j], win.at[j], ws.at[j], wr.at[j], along_z(j - 3))
+        return remote(red.at[j], win.at[j], ws.at[j], wr.at[j], along_z(-1 - j))
 
     def y_sum(j):
         for i in (1, 2, 3):
@@ -183,23 +189,38 @@
     for h in range(H):
         qs[h] = queries[:, h * DH : (h + 1) * DH]
     local[3].wait()
-    y_sum(0)
     ms[...] = jnp.full_like(ms, NEG)
     ls[...] = jnp.zeros_like(ls)
     acc[...] = jnp.zeros_like(acc)
     attend(0, 0, 0, ROWS, causal=True)
     attend(0, 1, HALF, HALF, causal=True)
+    known(0)
+    y_sum(0)
     arrived(1, 0)
+    known(1)
     y_sum(1)
     arrived(1, 1)
+    known(2)
     y_sum(2)
     arrived(2, 0)
     y_sum(3)
+    known(3)
+    known(4)
     arrived(2, 1)
+    known(5)
+    known(6)
     w_sum()
     arrived(3, 0)
     arrived(3, 1)
     arrived(4, 0)
+    local[4].wait()
+    arrived(4, 1)
+
+    heads = [(acc[h] / ls[h]).astype(BF16) for h in range(H)]
+    attended = jnp.concatenate(heads, axis=1)
+    final = jnp.dot(attended, wout[...], preferred_element_type=F32) + xin[...].astype(F32)
+    ov[...] = final.astype(BF16)
+
     for i in (5, 6, 7):
         local[i].wait()
     for i in range(1, 8):
@@ -213,14 +234,6 @@
     nma[...] = ma[...] - rate * update
     nmo[...] = new_moment
     nse[...] = new_second
-    local[4].wait()
-    arrived(4, 1)
-
-    heads = [(acc[h] / ls[h]).astype(BF16) for h in range(H)]
-    attended = jnp.concatenate(heads, axis=1)
-    final = jnp.dot(attended, wout[...], preferred_element_type=F32) + xin[...].astype(F32)
-    ov[...] = final.astype(BF16)
-
     for r in range(2):
         x_copy(r).wait_send()
     for j in range(4):
@@ -288,6 +301,7 @@
             dma((FAR, 2)), dma((FAR, 2)),
             dma((3,)), dma((3,)),
             dma((7,)), dma((7,)),
+            pltpu.SemaphoreType.REGULAR((7,)),
         ],
         compiler_params=pltpu.CompilerParams(
             collective_id=0, has_side_effects=True, vmem_limit_bytes=48 << 20

time: 88.2 us -> 79.9 us (0.906)
  the two profiles are of different devices: /device:TPU:152 before, /device:TPU:6 now
where the time goes in v3:
time: 79.9 us; the launch traced here: 79.7 us
  Pallas kernels  79.1 us (99%)
    pallas_call x1, Pallas kernels, on_device(): pl.pallas_call(kernel, out_shape=(vmem((ROWS, D), BF16), vmem(shard_rows,...  78.3 us

profile of v3, /device:TPU:6, one launch (start us, length us, event | category | flops | bytes accessed | tf_op | source)
XLA Modules:
  0.0 79.7 jit_solution(17369658229235087907)
XLA Ops:
  0.6 78.3 %shard_map.120 = (bf16[256,1024]{1,0:T(8,128)(2,1)S(1)}, f32[32,128]{1,0:T(8,128)S(1)}, f32[32,128]{1,0:T(8,128)S(1)}, f32[32,128]{1,0:T(8,128)S(1)}) custom-call(bf16[256,1024]{1,0:T(8,128)(2,1)} %bitcast.15, s32[16,128]{1,0:T(8,128)} %bitcast.19, f32[1,1024]{1,0:T(1,128)} %gain_hbm.1, bf16[1024,1536]{1,0:T(8,128)(2,1)} %bitcast.12, ...), custom_call_target="tpu_custom_call" | custom-call | tf_op jit(solution)/shard_map/pallas_call | solution.py:267
  78.9 0.8 %shard_map.121 = (bf16[256,1024]{1,0:T(8,128)(2,1)}, f32[32,128]{1,0:T(8,128)}, f32[32,128]{1,0:T(8,128)}, f32[32,128]{1,0:T(8,128)}) custom-call(bf16[256,1024]{1,0:T(8,128)(2,1)S(1)} %get-tuple-element.12.refs_0_, f32[32,128]{1,0:T(8,128)S(1)} %get-tuple-element.13.refs_1_, f32[32,128]{1,0:T(8,128)S(1)} %get-tuple-element.14.refs_2_, ...), custom_call_target="tpu_custom_call" | custom-call | tf_op jit(solution)/shard_map/pallas_call | solution.py:322

commit v4 on v3

--- a/solution.py
+++ b/solution.py
@@ -13,8 +13,6 @@
 ROWS = 256
 HALF = 128
 HC = H * DH
-FAR_ORDER = (4, 3, 5, 2, 6, 1, 7)
-FAR = 4
 NEG = -1e30
 
 eps_norm = 1e-06
@@ -34,9 +32,9 @@
 def kernel(
     x_hbm, seg_hbm, gain_hbm, wqkv_hbm, wout_hbm, g_hbm, ma_hbm, mo_hbm, se_hbm,
     ov, nma, nmo, nse,
-    xin, nrm, wqkv, wout, gain, seg, segq, kv, qs, acc, ms, ls,
-    g, yin, red, win, far, ma, mo, se,
-    loc, xs, xr, ys, yr, ks, kr, ws, wr, fs, fr, said,
+    xin, nrm, wqkv, wout, gain, seg, segk, segq, kv, qs, acc, ms, ls, part, stat,
+    g, gb, yin, red, sent, win, far, ma, mo, se,
+    loc, xs, xr, ys, yr, ks, kr, qss, qrs, ps, pr, ws, wr, fs, fr, said,
 ):
     p, c, d = lax.axis_index("pipe"), lax.axis_index("ctx"), lax.axis_index("dp")
     zh, y = lax.div(d, 4), lax.rem(d, 4)
@@ -50,7 +48,7 @@
         at = lax.rem(z + by + 32, 32)
         return p, lax.rem(at, 8), lax.div(at, 8) * 4 + y
 
-    up = along_z(1)
+    up, down = along_z(1), along_z(-1)
 
     def remote(src, dst, ssem, rsem, dev):
         return pltpu.make_async_remote_copy(
@@ -70,7 +68,12 @@
     barrier = pltpu.get_barrier_semaphore()
     for dev in (prv, along_y(1), along_y(2), along_y(3), along_z(-1)):
         pl.semaphore_signal(barrier, inc=1, device_id=dev, device_id_type=MESH)
-    pl.semaphore_wait(barrier, 5)
+
+    @pl.when((c >= 2) & (c < 7))
+    def _():
+        pl.semaphore_signal(barrier, inc=1, device_id=up, device_id_type=MESH)
+
+    pl.semaphore_wait(barrier, 5 + (c >= 3).astype(jnp.int32))
     pl.semaphore_signal(said.at[0], inc=1, device_id=up, device_id_type=MESH)
 
     def known(i):
@@ -87,15 +90,18 @@
     def group(j):
         return lax.rem(z + 3 - j, 4)
 
-    def y_copy(j, i):
-        src = g_hbm.at[:, group(j), :, lax.rem(y + i, 4)]
-        return remote(src, yin.at[j, i - 1], ys.at[j, i - 1], yr.at[j, i - 1], along_y(i))
+    def y_copy(u, j, i):
+        src = gb.at[u, group(j), :, lax.rem(y + i, 4)]
+        return remote(src, yin.at[u, j, i - 1], ys.at[u, j, i - 1], yr.at[u, j, i - 1], along_y(i))
 
     for r in range(2):
         x_copy(r).start()
-    for j in range(4):
-        for i in (1, 2, 3):
-            y_copy(j, i).start()
+    local[3].wait()
+    for u in range(2):
+        for j in range(4):
+            gb[u, group(j)] = g[u, group(j)].astype(BF16)
+            for i in (1, 2, 3):
+                y_copy(u, j, i).start()
 
     def kv_copy(k, r):
         return remote(kv.at[k, r], kv.at[k + 1, r], ks.at[k, r], kr.at[k, r], up)
@@ -116,118 +122,229 @@
         def _():
             kv_copy(0, r).start()
 
-
-    def attend(k, r, q0, qn, causal=False):
-        rows = pl.ds(q0, qn)
-        keyseg = seg[pl.ds(2 * (c - k) + r, 1), :]
-        mask = segq[rows, :] == keyseg
-        if causal:
-            place = lax.broadcasted_iota(jnp.int32, (qn, HALF), 0) + q0
-            mask = mask & (lax.broadcasted_iota(jnp.int32, (qn, HALF), 1) + r * HALF <= place)
+    def q_copy(i):
+        return remote(qs.at[i], qs.at[i + 1], qss.at[i], qrs.at[i], down)
+
+
+    def attend(i, k, r):
+        mask = segk[k, r] == segq[i]
+        if k == 0:
+            place = lax.broadcasted_iota(jnp.int32, (HALF, ROWS), 0) + r * HALF
+            mask = mask & (place <= lax.broadcasted_iota(jnp.int32, (HALF, ROWS), 1))
+        first = (i > 0 or k == 0) and r == 0
         for h in range(H):
             s = lax.dot_general(
-                qs[h, rows, :], kv[k, r, 0, h], (((1,), (1,)), ((), ())), preferred_element_type=F32
+                kv[k, r, 0, h], qs[i, h], (((1,), (1,)), ((), ())), preferred_element_type=F32
             )
             s = jnp.where(mask, s * (DH ** (-0.5)), NEG)
-            old = ms[h, rows, :]
-            top = jnp.maximum(old, jnp.max(s, axis=-1, keepdims=True))
+            top = jnp.max(s, axis=0, keepdims=True)
+            if not first:
+                old = ms[i, h]
+                top = jnp.maximum(old, top)
             w = jnp.exp(s - top)
-            shrink = jnp.exp(old - top)
-            ms[h, rows, :] = top
-            ls[h, rows, :] = shrink * ls[h, rows, :] + jnp.sum(w, axis=-1, keepdims=True)
-            acc[h, rows, :] = shrink * acc[h, rows, :] + jnp.dot(
-                w.astype(BF16), kv[k, r, 1, h], preferred_element_type=F32
+            total = jnp.sum(w, axis=0, keepdims=True)
+            value = lax.dot_general(
+                kv[k, r, 1, h], w.astype(BF16), (((0,), (0,)), ((), ())), preferred_element_type=F32
             )
-
-    def arrived(k, r):
+            if not first:
+                shrink = jnp.exp(old - top)
+                total = total + shrink * ls[i, h]
+                value = value + shrink * acc[i, h]
+            ms[i, h] = top
+            ls[i, h] = total
+            acc[i, h] = value
+
+    def kv_arrived(k, r):
         @pl.when(c >= k)
         def _():
             kv_copy(k - 1, r).wait_recv()
 
-        if k < FAR:
-            @pl.when((c >= k) & (c < 7))
+        if k == 1:
+            @pl.when((c >= 1) & (c < 7))
             def _():
-                kv_copy(k, r).start()
+                kv_copy(1, r).start()
 
         @pl.when(c >= k)
         def _():
-            if k == FAR and r == 0:
-                attend(k, r, 0, HALF)
-            else:
-                attend(k, r, 0, ROWS)
-
-    def w_copy(j):
-        return remote(red.at[j], win.at[j], ws.at[j], wr.at[j], along_z(-1 - j))
-
-    def y_sum(j):
+            attend(0, k, r)
+
+    def part_copy(n, u):
+        return (
+            remote(part.at[n, u], part.at[n + 1, u], ps.at[n // 2, u, 0], pr.at[n // 2, u, 0], up),
+            remote(stat.at[n, u], stat.at[n + 1, u], ps.at[n // 2, u, 1], pr.at[n // 2, u, 1], up),
+        )
+
+    def merged(i, n, h):
+        u, v = divmod(h, 2)
+        m, t = stat[n, u, 2 * v : 2 * v + 1, :], stat[n, u, 2 * v + 1 : 2 * v + 2, :]
+        top = jnp.maximum(ms[i, h], m)
+        mine, other = jnp.exp(ms[i, h] - top), t * jnp.exp(m - top)
+        ms[i, h] = top
+        ls[i, h] = mine * ls[i, h] + other
+        acc[i, h] = mine * acc[i, h] + other * part[n, u, v].astype(F32)
+
+    def send_part(i, n, u):
+        for v in range(2):
+            h = 2 * u + v
+            part[n, u, v] = (acc[i, h] / ls[i, h]).astype(BF16)
+            stat[n, u, 2 * v : 2 * v + 1, :] = ms[i, h]
+            stat[n, u, 2 * v + 1 : 2 * v + 2, :] = ls[i, h]
+        for one in part_copy(n, u):
+            one.start()
+
+    def take_part(i, n, u):
+        for one in part_copy(n - 1, u):
+            one.wait_recv()
+        for v in range(2):
+            merged(i, n, 2 * u + v)
+
+    def w_copy(u, j):
+        return remote(sent.at[u, j], win.at[u, j], ws.at[u, j], wr.at[u, j], along_z(-1 - j))
+
+    def y_sum(u, j):
         for i in (1, 2, 3):
-            y_copy(j, i).wait_recv()
-        red[j] = g[:, group(j), :, y] + yin[j, 0] + yin[j, 1] + yin[j, 2]
+            y_copy(u, j, i).wait_recv()
+        total = g[u, group(j), :, y]
+        for i in range(3):
+            total = total + yin[u, j, i].astype(F32)
+        if j == 3:
+            red[u] = total
+        else:
+            sent[u, j] = total.astype(BF16)
         if j < 3:
-            w_copy(j).start()
+            w_copy(u, j).start()
 
     def f_copy(i):
         at = lax.rem(z + 32 - 4 * i, 32)
-        src = red.at[3, lax.div(lax.rem(at, 8), 4), lax.div(at, 8)]
+        src = sent.at[lax.div(lax.rem(at, 8), 4), 3, lax.div(at, 8)]
         return remote(src, far.at[i - 1], fs.at[i - 1], fr.at[i - 1], along_z(-4 * i))
 
-    def w_sum():
+    def w_sum(u):
         for j in range(3):
-            w_copy(j).wait_recv()
-        red[3] = red[3] + win[0] + win[1] + win[2]
-        for i in FAR_ORDER:
-            f_copy(i).start()
+            w_copy(u, j).wait_recv()
+        total = red[u]
+        for j in range(3):
+            total = total + win[u, j].astype(F32)
+        red[u] = total
+        sent[u, 3] = total.astype(BF16)
+
+        @pl.when(lax.div(c, 4) == u)
+        def _():
+            for i in (4, 2, 6):
+                f_copy(i).start()
+
+        @pl.when(lax.div(c, 4) != u)
+        def _():
+            for i in (3, 5, 1, 7):
+                f_copy(i).start()
 
     for i in (0, 1, 2):
         local[i].wait()
     project(0)
-    for r in range(2):
-        cols = jnp.broadcast_to(seg[pl.ds(2 * c + r, 1), :], (HALF, HALF))
-        segq[pl.ds(r * HALF, HALF), :] = jnp.transpose(cols)
     project(1)
     queries = jnp.dot(nrm[...], wqkv[:, :HC], preferred_element_type=F32).astype(BF16)
     for h in range(H):
-        qs[h] = queries[:, h * DH : (h + 1) * DH]
-    local[3].wait()
-    ms[...] = jnp.full_like(ms, NEG)
-    ls[...] = jnp.zeros_like(ls)
-    acc[...] = jnp.zeros_like(acc)
-    attend(0, 0, 0, ROWS, causal=True)
-    attend(0, 1, HALF, HALF, causal=True)
+        qs[0, h] = queries[:, h * DH : (h + 1) * DH]
+
+    @pl.when(c >= 3)
+    def _():
+        q_copy(0).start()
+
+    for k in range(3):
+        for r in range(2):
+            at = jnp.maximum(2 * (c - k) + r, 0)
+            cols = jnp.transpose(jnp.broadcast_to(seg[pl.ds(at, 1), :], (HALF, HALF)))
+            segk[k, r] = jnp.concatenate([cols, cols], axis=1)
+    for i in range(3):
+        at = 2 * jnp.minimum(c + i, 7)
+        segq[i] = jnp.concatenate([seg[pl.ds(at, 1), :], seg[pl.ds(at + 1, 1), :]], axis=1)
+    attend(0, 0, 0)
+    attend(0, 0, 1)
     known(0)
-    y_sum(0)
-    arrived(1, 0)
+    y_sum(0, 0)
     known(1)
-    y_sum(1)
-    arrived(1, 1)
+    y_sum(0, 1)
     known(2)
-    y_sum(2)
-    arrived(2, 0)
-    y_sum(3)
+    y_sum(0, 2)
+    kv_arrived(1, 0)
+    y_sum(0, 3)
     known(3)
+
+    @pl.when((c >= 2) & (c < 7))
+    def _():
+        q_copy(0).wait_recv()
+
+    @pl.when((c >= 3) & (c < 7))
+    def _():
+        q_copy(1).start()
+
+    y_sum(1, 0)
+    kv_arrived(1, 1)
     known(4)
-    arrived(2, 1)
+    y_sum(1, 1)
     known(5)
+    y_sum(1, 2)
     known(6)
-    w_sum()
-    arrived(3, 0)
-    arrived(3, 1)
-    arrived(4, 0)
+    w_sum(0)
+    y_sum(1, 3)
+    kv_arrived(2, 0)
+
+    @pl.when((c >= 2) & (c < 7))
+    def _():
+        attend(1, 2, 0)
+
+    @pl.when((c >= 2) & (c < 6))
+    def _():
+        q_copy(1).wait_recv()
+        attend(2, 2, 0)
+
+    w_sum(1)
+
+    @pl.when(c >= 2)
+    def _():
+        kv_copy(1, 1).wait_recv()
+
+    @pl.when((c >= 2) & (c < 6))
+    def _():
+        attend(2, 2, 1)
+        send_part(2, 0, 0)
+        send_part(2, 0, 1)
+
+    @pl.when((c >= 2) & (c < 7))
+    def _():
+        attend(1, 2, 1)
+
+    for u in range(2):
+        @pl.when((c >= 3) & (c < 7))
+        def _():
+            take_part(1, 1, u)
+
+        @pl.when((c >= 2) & (c < 7))
+        def _():
+            send_part(1, 2, u)
+
+        if u == 0:
+            @pl.when(c >= 2)
+            def _():
+                attend(0, 2, 1)
+
     local[4].wait()
-    arrived(4, 1)
-
-    heads = [(acc[h] / ls[h]).astype(BF16) for h in range(H)]
-    attended = jnp.concatenate(heads, axis=1)
-    final = jnp.dot(attended, wout[...], preferred_element_type=F32) + xin[...].astype(F32)
-    ov[...] = final.astype(BF16)
+    for u in range(2):
+        @pl.when(c >= 3)
+        def _():
+            take_part(0, 3, u)
+
+    attended = jnp.concatenate([(acc[0, h] / ls[0, h]).astype(BF16) for h in range(H)], axis=0)
+    final = lax.dot_general(attended, wout[...], (((0,), (0,)), ((), ())), preferred_element_type=F32)
+    ov[...] = (final + xin[...].astype(F32)).astype(BF16)
 
     for i in (5, 6, 7):
         local[i].wait()
     for i in range(1, 8):
         f_copy(i).wait_recv()
-    grad = red[3, lax.div(c, 4), zh]
+    grad = red[lax.div(c, 4), zh]
     for i in range(7):
-        grad = grad + far[i]
+        grad = grad + far[i].astype(F32)
     new_moment = beta_one * mo[...] + (1.0 - beta_one) * grad
     new_second = beta_two * se[...] + (1.0 - beta_two) * grad * grad
     update = new_moment / fix_one / (jnp.sqrt(new_second / fix_two) + adam_eps) + decay * ma[...]
@@ -236,18 +353,34 @@
     nse[...] = new_second
     for r in range(2):
         x_copy(r).wait_send()
-    for j in range(4):
-        for i in (1, 2, 3):
-            y_copy(j, i).wait_send()
-    for j in range(3):
-        w_copy(j).wait_send()
+    for u in range(2):
+        for j in range(4):
+            for i in (1, 2, 3):
+                y_copy(u, j, i).wait_send()
+        for j in range(3):
+            w_copy(u, j).wait_send()
     for i in range(1, 8):
         f_copy(i).wait_send()
-    for k in range(FAR):
+    for k in range(2):
         @pl.when((c >= k) & (c < 7))
         def _():
             for r in range(2):
                 kv_copy(k, r).wait_send()
+
+    @pl.when(c >= 3)
+    def _():
+        q_copy(0).wait_send()
+
+    @pl.when((c >= 3) & (c < 7))
+    def _():
+        q_copy(1).wait_send()
+
+    for n, last in ((0, 6), (2, 7)):
+        @pl.when((c >= 2) & (c < last))
+        def _():
+            for u in range(2):
+                for one in part_copy(n, u):
+                    one.wait_send()
 
 
 def hand_over(*refs):
@@ -281,25 +414,32 @@
             vmem((HC, D), BF16),
             vmem((1, D), F32),
             vmem((16, 128), jnp.int32),
-            vmem((ROWS, HALF), jnp.int32),
-            vmem((FAR + 1, 2, 2, H, HALF, DH), BF16),
-            vmem((H, ROWS, DH), BF16),
-            vmem((H, ROWS, DH), F32),
-            vmem((H, ROWS, DH), F32),
-            vmem((H, ROWS, DH), F32),
+            vmem((3, 2, HALF, ROWS), jnp.int32),
+            vmem((3, 1, ROWS), jnp.int32),
+            vmem((3, 2, 2, H, HALF, DH), BF16),
+            vmem((3, H, ROWS, DH), BF16),
+            vmem((3, H, DH, ROWS), F32),
+            vmem((3, H, 1, ROWS), F32),
+            vmem((3, H, 1, ROWS), F32),
+            vmem((4, 2, 2, DH, ROWS), BF16),
+            vmem((4, 2, 4, ROWS), F32),
             vmem((2, 4, 4, 4, 32, 128), F32),
-            vmem((4, 3, 2, 4, 32, 128), F32),
-            vmem((4, 2, 4, 32, 128), F32),
-            vmem((3, 2, 4, 32, 128), F32),
-            vmem((7, 32, 128), F32),
+            vmem((2, 4, 4, 4, 32, 128), BF16),
+            vmem((2, 4, 3, 4, 32, 128), BF16),
+            vmem((2, 4, 32, 128), F32),
+            vmem((2, 4, 4, 32, 128), BF16),
+            vmem((2, 3, 4, 32, 128), BF16),
+            vmem((7, 32, 128), BF16),
             vmem(shard_rows, F32),
             vmem(shard_rows, F32),
             vmem(shard_rows, F32),
             dma((8,)),
             dma((2,)), dma((2,)),
-            dma((4, 3)), dma((4, 3)),
-            dma((FAR, 2)), dma((FAR, 2)),
-            dma((3,)), dma((3,)),
+            dma((2, 4, 3)), dma((2, 4, 3)),
+            dma((2, 2)), dma((2, 2)),
+            dma((2,)), dma((2,)),
+            dma((2, 2, 2)), dma((2, 2, 2)),
+            dma((2, 3)), dma((2, 3)),
             dma((7,)), dma((7,)),
             pltpu.SemaphoreType.REGULAR((7,)),
         ],

time: 79.9 us -> 66.1 us (0.83)
  the two profiles are of different devices: /device:TPU:6 before, /device:TPU:64 now
where the time goes in v4:
time: 66.1 us; the launch traced here: 66 us
  Pallas kernels  65.3 us (99%)
    pallas_call x1, Pallas kernels, on_device(): pl.pallas_call(kernel, out_shape=(vmem((ROWS, D), BF16), vmem(shard_rows,...  64.5 us

profile of v4, /device:TPU:64, one launch (start us, length us, event | category | flops | bytes accessed | tf_op | source)
XLA Modules:
  0.0 66.0 jit_solution(16701559938475554969)
XLA Ops:
  0.6 64.5 %shard_map.120 = (bf16[256,1024]{1,0:T(8,128)(2,1)S(1)}, f32[32,128]{1,0:T(8,128)S(1)}, f32[32,128]{1,0:T(8,128)S(1)}, f32[32,128]{1,0:T(8,128)S(1)}) custom-call(bf16[256,1024]{1,0:T(8,128)(2,1)} %bitcast.15, s32[16,128]{1,0:T(8,128)} %bitcast.19, f32[1,1024]{1,0:T(1,128)} %gain_hbm.1, bf16[1024,1536]{1,0:T(8,128)(2,1)} %bitcast.12, ...), custom_call_target="tpu_custom_call" | custom-call | tf_op jit(solution)/shard_map/pallas_call | solution.py:400
  65.1 0.8 %shard_map.121 = (bf16[256,1024]{1,0:T(8,128)(2,1)}, f32[32,128]{1,0:T(8,128)}, f32[32,128]{1,0:T(8,128)}, f32[32,128]{1,0:T(8,128)}) custom-call(bf16[256,1024]{1,0:T(8,128)(2,1)S(1)} %get-tuple-element.12.refs_0_, f32[32,128]{1,0:T(8,128)S(1)} %get-tuple-element.13.refs_1_, f32[32,128]{1,0:T(8,128)S(1)} %get-tuple-element.14.refs_2_, ...), custom_call_target="tpu_custom_call" | custom-call | tf_op jit(solution)/shard_map/pallas_call | solution.py:462

commit v5 on v4

--- a/solution.py
+++ b/solution.py
@@ -258,48 +258,47 @@
     for i in range(3):
         at = 2 * jnp.minimum(c + i, 7)
         segq[i] = jnp.concatenate([seg[pl.ds(at, 1), :], seg[pl.ds(at + 1, 1), :]], axis=1)
-    attend(0, 0, 0)
-    attend(0, 0, 1)
     known(0)
     y_sum(0, 0)
     known(1)
     y_sum(0, 1)
     known(2)
     y_sum(0, 2)
+    y_sum(0, 3)
+    attend(0, 0, 0)
+    attend(0, 0, 1)
+    known(3)
+    y_sum(1, 0)
     kv_arrived(1, 0)
-    y_sum(0, 3)
-    known(3)
-
-    @pl.when((c >= 2) & (c < 7))
-    def _():
-        q_copy(0).wait_recv()
-
-    @pl.when((c >= 3) & (c < 7))
-    def _():
-        q_copy(1).start()
-
-    y_sum(1, 0)
-    kv_arrived(1, 1)
     known(4)
     y_sum(1, 1)
+    y_sum(1, 2)
+
+    @pl.when((c >= 2) & (c < 7))
+    def _():
+        q_copy(0).wait_recv()
+
+    @pl.when((c >= 3) & (c < 7))
+    def _():
+        q_copy(1).start()
+
     known(5)
-    y_sum(1, 2)
+    y_sum(1, 3)
+    kv_arrived(1, 1)
+    kv_arrived(2, 0)
+
+    @pl.when((c >= 2) & (c < 7))
+    def _():
+        attend(1, 2, 0)
+
+    @pl.when((c >= 2) & (c < 6))
+    def _():
+        q_copy(1).wait_recv()
+        attend(2, 2, 0)
+
     known(6)
     w_sum(0)
-    y_sum(1, 3)
-    kv_arrived(2, 0)
-
-    @pl.when((c >= 2) & (c < 7))
-    def _():
-        attend(1, 2, 0)
-
-    @pl.when((c >= 2) & (c < 6))
-    def _():
-        q_copy(1).wait_recv()
-        attend(2, 2, 0)
-
     w_sum(1)
-
     @pl.when(c >= 2)
     def _():
         kv_copy(1, 1).wait_recv()

time: 66.1 us -> 64.3 us (0.973)
  the two profiles are of different devices: /device:TPU:64 before, /device:TPU:72 now
where the time goes in v5:
time: 64.3 us; the launch traced here: 64.1 us
  Pallas kernels  63.5 us (99%)
    pallas_call x1, Pallas kernels, on_device(): pl.pallas_call(kernel, out_shape=(vmem((ROWS, D), BF16), vmem(shard_rows,...  62.7 us

profile of v5, /device:TPU:72, one launch (start us, length us, event | category | flops | bytes accessed | tf_op | source)
XLA Modules:
  0.0 64.1 jit_solution(13137471802438123816)
XLA Ops:
  0.6 62.7 %shard_map.120 = (bf16[256,1024]{1,0:T(8,128)(2,1)S(1)}, f32[32,128]{1,0:T(8,128)S(1)}, f32[32,128]{1,0:T(8,128)S(1)}, f32[32,128]{1,0:T(8,128)S(1)}) custom-call(bf16[256,1024]{1,0:T(8,128)(2,1)} %bitcast.15, s32[16,128]{1,0:T(8,128)} %bitcast.19, f32[1,1024]{1,0:T(1,128)} %gain_hbm.1, bf16[1024,1536]{1,0:T(8,128)(2,1)} %bitcast.12, ...), custom_call_target="tpu_custom_call" | custom-call | tf_op jit(solution)/shard_map/pallas_call | solution.py:399
  63.3 0.8 %shard_map.121 = (bf16[256,1024]{1,0:T(8,128)(2,1)}, f32[32,128]{1,0:T(8,128)}, f32[32,128]{1,0:T(8,128)}, f32[32,128]{1,0:T(8,128)}) custom-call(bf16[256,1024]{1,0:T(8,128)(2,1)S(1)} %get-tuple-element.12.refs_0_, f32[32,128]{1,0:T(8,128)S(1)} %get-tuple-element.13.refs_1_, f32[32,128]{1,0:T(8,128)S(1)} %get-tuple-element.14.refs_2_, ...), custom_call_target="tpu_custom_call" | custom-call | tf_op jit(solution)/shard_map/pallas_call | solution.py:461
